TPU v7x, 1024 devices: a whole 8x8x8 slice. The times are simulated.
1024 devices in a mesh: section: 8 (over y), expert: 16 (over z, core), tensor: 8 (over x).
Axes of the slice: x: 8, y: 8, z: 8, core: 2. Of those that a mesh axis runs over, the one named last changes fastest.
Arguments:
- tokens: bfloat16 [8, 16384, 2048], P('section', ('expert', 'tensor')), may hold values from -6 to 6
- routes: int32 [8, 16384, 2], P('section', ('expert', 'tensor')), may hold values from 0 to 15, all different within a row; in each aligned block of 128 rows (0 to 127, 128 to 255, ..., all dimensions but the last counted through in order) at most 32 rows name the same one
- route_weights: float32 [8, 16384, 2], P('section', ('expert', 'tensor')), may hold values from 0.2 to 1
- expert_gate: bfloat16 [8, 16, 2048, 512], P('section', 'expert'), may hold values from -0.125 to 0.125
- expert_up: bfloat16 [8, 16, 2048, 512], P('section', 'expert'), may hold values from -0.125 to 0.125
- expert_down: bfloat16 [8, 16, 512, 2048], P('section', 'expert'), may hold values from -0.25 to 0.25
Outputs:
- layer_out: bfloat16 [8, 16384, 2048], P('section', ('expert', 'tensor'))
- next_input: bfloat16 [8, 16384, 2048], P('section', ('expert', 'tensor'))
Inputs may be any that keep to these rules, and one draw needn't show every extreme that they name: Each token names 2 different experts; among the tokens of one device no expert is named by more than 32 routes, a bound that some block reaches.
All inputs are finite; a program needn't handle non-finite values.
Results may differ from a plain program's by a relative error of at most 0.0042.
Values may be sent and summed in bfloat16 or wider, within the bound.
A program may use at most 32 MiB of HBM per device.

v0:
```python
import jax
import jax.numpy as jnp
from jax import lax
from jax.sharding import PartitionSpec as P


def passed_along(value, axis, steps):
    count = lax.axis_size(axis)
    leading, last = (max(0, -steps), min(count, count - steps))
    return lax.ppermute(value, axis, [(source, source + steps) for source in range(leading, last)])


def per_device(tokens, routes, route_weights, expert_gate, expert_up, expert_down):
    rows_in = tokens[0]
    tok_count, width = rows_in.shape
    top_count = routes.shape[2]
    flat_routes = routes[0].reshape(tok_count * top_count)
    flat_weights = route_weights[0].reshape(tok_count * top_count)
    n_expert = lax.axis_size("expert")
    exp_dev = expert_gate.shape[1]
    expert_count = exp_dev * n_expert
    capacity = max(2, 2 * tok_count * top_count // expert_count)
    onehot = (flat_routes[:, None] == jnp.arange(expert_count, dtype=jnp.int32)[None, :]).astype(
        jnp.int32
    )
    ranked = jnp.sum((jnp.cumsum(onehot, axis=0) - 1) * onehot, axis=1)
    slot_index = flat_routes * capacity + ranked
    token_of = jnp.arange(tok_count * top_count, dtype=jnp.int32) // top_count
    outgoing = (
        jnp.zeros((expert_count * capacity, width), jnp.bfloat16)
        .at[slot_index]
        .set(rows_in[token_of])
    )
    outgoing = outgoing.reshape(n_expert, exp_dev, capacity, width)
    arrived = lax.all_to_all(outgoing, "expert", split_axis=0, concat_axis=2, tiled=True)
    slot_rows = arrived[0]
    gate_val = jnp.einsum(
        "esd,edf->esf", slot_rows, expert_gate[0], preferred_element_type=jnp.float32
    )
    up_val = jnp.einsum("esd,edf->esf", slot_rows, expert_up[0], preferred_element_type=jnp.float32)
    hidden = (jax.nn.silu(gate_val) * up_val).astype(jnp.bfloat16)
    expert_out = jnp.einsum(
        "esf,efd->esd", hidden, expert_down[0], preferred_element_type=jnp.float32
    ).astype(jnp.bfloat16)
    expert_out = expert_out.reshape(exp_dev, n_expert, capacity, width)
    came_back = lax.all_to_all(expert_out, "expert", split_axis=1, concat_axis=0, tiled=True)
    back_rows = came_back.reshape(expert_count * capacity, width)
    picked = back_rows[slot_index].astype(jnp.float32) * flat_weights[:, None]
    routed = jnp.sum(picked.reshape(tok_count, top_count, width), axis=1)
    layer_out = (rows_in.astype(jnp.float32) + routed).astype(jnp.bfloat16)
    handed = passed_along(layer_out, "section", 1)
    return (layer_out[None], handed[None])


def solution(mesh):
    in_specs = (
        P("section", ("expert", "tensor"), None),
        P("section", ("expert", "tensor"), None),
        P("section", ("expert", "tensor"), None),
        P("section", "expert", None, None),
        P("section", "expert", None, None),
        P("section", "expert", None, None),
    )
    out_specs = (P("section", ("expert", "tensor"), None), P("section", ("expert", "tensor"), None))
    return jax.shard_map(
        per_device, mesh=mesh, in_specs=in_specs, out_specs=out_specs, check_vma=False
    )
```

profile of v0, /device:TPU:64, one launch (start us, length us, event | category | flops | bytes accessed | tf_op | source)
XLA Modules:
  0.0 169.2 jit_solution(11610871853956248163)
XLA Ops:
  0.6 0.0 copy-start
  0.6 0.9 copy.15
  1.6 0.1 eq.29
  1.7 0.1 eq.25
  1.9 0.7 broadcast_multiply_fusion
  2.6 0.6 reduce-window.6
  3.2 0.2 slice_reduce_fusion
  3.4 0.1 copy.14
  3.5 0.1 mul.41
  3.7 0.1 fusion.19
  3.8 7.4 %scatter_custom_fusion = bf16[512,2048]{1,0:T(8,128)(2,1)} fusion(s32[256]{0:T(256)S(1)} %bitcast.55, bf16[128,2048]{1,0:T(8,128)(2,1)} %bitcast.53, s32[1024]{0:T(1024)S(1)} %pad_clamp_fusion.1, bf16[]{:T(256)} %constant.28.clone.1), kind=kCustom, calls=%fused_computation.14 | custom fusion | bytes 2097664 | tf_op jit(solution)/shard_map/scatter | solution.py:32
  11.1 0.0 copy-start.4
  11.1 66.6 %all_to_all.8 = bf16[16,1,32,2048]{3,2,1,0:T(8,128)(2,1)S(1)} all-to-all(bf16[16,1,32,2048]{3,2,1,0:T(8,128)(2,1)} %bitcast.49), channel_id=1, replica_groups=mesh['section'=8,'expert'=16,'tensor'=8] {'expert'}, dimensions={0} | all-to-all | bytes 4194304 | tf_op jit(solution)/shard_map/all_to_all | solution.py:35
  77.8 0.0 copy-start.1
  77.8 1.3 copy-done.1
  79.1 0.0 copy-done.4
  79.1 1.2 fusion.3
  80.3 0.0 copy-done
  80.3 6.1 %convolution_convert_fusion = bf16[512,2048]{1,0:T(8,128)(2,1)} fusion(bf16[1,1,512,2048]{3,2,1,0:T(8,128)(2,1)S(1)} %copy-done, bf16[512,2048]{1,0:T(8,128)(2,1)} %bitcast.52, bf16[1,1,2048,512]{3,2,1,0:T(8,128)(2,1)} %param.10, f32[512,512]{1,0:T(8,128)S(1)} %fusion.3), kind=kOutput, calls=%fused_computation.3 | convolution fusion | flops 2150105088 | bytes 9437184 | tf_op jit(solution)/shard_map/esf,efd->esd/dot_general | solution.py:42
  86.4 0.0 copy-start.3
  86.4 4.8 %all-to-all-start.1 = ((bf16[1,16,32,2048]{3,2,0,1:T(8,128)(2,1)}), bf16[1,16,32,2048]{3,2,0,1:T(8,128)(2,1)}, u32[]{:S(2)}, u32[]{:S(2)}) async-start(bf16[1,16,32,2048]{3,2,0,1:T(8,128)(2,1)} %bitcast.50), calls=%async_computation.1 | async-start | bytes 4194304 | tf_op jit(solution)/shard_map/all_to_all | solution.py:46
  91.2 0.0 copy-done.3
  91.2 0.1 copy.19
  91.3 49.0 %all-to-all-done.1 = bf16[1,16,32,2048]{3,2,0,1:T(8,128)(2,1)} async-done(((bf16[1,16,32,2048]{3,2,0,1:T(8,128)(2,1)}), bf16[1,16,32,2048]{3,2,0,1:T(8,128)(2,1)}, u32[]{:S(2)}, u32[]{:S(2)}) %all-to-all-start.1) | async-done | bytes 2097184 | tf_op jit(solution)/shard_map/all_to_all | solution.py:46
  140.3 4.2 %gather_fusion = bf16[256,2048]{1,0:T(8,128)(2,1)S(1)} fusion(bf16[512,2048]{1,0:T(8,128)(2,1)} %bitcast.12, s32[1024]{0:T(1024)S(1)} %pad_clamp_fusion), kind=kCustom, calls=%fused_computation.1 | custom fusion | bytes 2098176 | tf_op jit(solution)/shard_map/gather | solution.py:48
  144.5 2.4 %reshape.162 = f32[128,2,2048]{2,1,0:T(2,128)} reshape(bf16[256,2048]{1,0:T(8,128)(2,1)S(1)} %gather_fusion) | data formatting | bytes 3145728 | tf_op jit(solution)/shard_map/convert_element_type | solution.py:48
  146.9 0.0 copy-start.2
  146.9 4.9 %multiply_reduce_fusion = f32[128,2048]{1,0:T(8,128)S(1)} fusion(f32[128,2,2048]{2,1,0:T(2,128)} %reshape.162, f32[128,2]{1,0:T(8,128)S(1)} %copy.19), kind=kLoop, calls=%fused_computation.9 | loop fusion | flops 786432 | bytes 3146752 | tf_op jit(solution)/shard_map/reduce_sum | solution.py:49
  151.7 0.0 copy-done.2
  151.8 0.1 add_convert_fusion
  151.9 2.7 %collective-permute-start = (bf16[128,2048]{1,0:T(8,128)(2,1)S(1)}, bf16[128,2048]{1,0:T(8,128)(2,1)S(1)}, u32[]{:S(2)}, u32[]{:S(2)}) collective-permute-start(bf16[128,2048]{1,0:T(8,128)(2,1)S(1)} %add_convert_fusion), channel_id=1, source_target_pairs={{0,128},{128,256},{256,384},{384,512},{512,640},{640,768},{768,896... | collective-permute-start | bytes 1572872 | tf_op jit(solution)/shard_map/ppermute | solution.py:10
  154.6 0.9 fusion.11
  155.5 13.0 %collective-permute-done = bf16[128,2048]{1,0:T(8,128)(2,1)S(1)} collective-permute-done((bf16[128,2048]{1,0:T(8,128)(2,1)S(1)}, bf16[128,2048]{1,0:T(8,128)(2,1)S(1)}, u32[]{:S(2)}, u32[]{:S(2)}) %collective-permute-start) | collective-permute-done | bytes 524320 | tf_op jit(solution)/shard_map/ppermute | solution.py:10
  168.4 0.8 copy.23
  (7 shorter events, 0.1 us)
Async XLA Ops:
  0.6 79.7 %copy-start = (bf16[1,1,512,2048]{3,2,1,0:T(8,128)(2,1)S(1)}, bf16[1,1,512,2048]{3,2,1,0:T(8,128)(2,1)}, u32[]{:S(2)}) copy-start(bf16[1,1,512,2048]{3,2,1,0:T(8,128)(2,1)} %param.11) | copy-start | bytes 6291460
  11.1 67.9 %copy-start.4 = (bf16[1,1,2048,512]{3,2,1,0:T(8,128)(2,1)S(1)}, bf16[1,1,2048,512]{3,2,1,0:T(8,128)(2,1)}, u32[]{:S(2)}) copy-start(bf16[1,1,2048,512]{3,2,1,0:T(8,128)(2,1)} %param.9) | copy-start | bytes 6291460
  77.8 1.3 copy-start.1
  86.4 4.8 %copy-start.3 = (f32[1,128,2]{1,2,0:T(2,128)S(1)}, f32[1,128,2]{1,2,0:T(2,128)}, u32[]{:S(2)}) copy-start(f32[1,128,2]{1,2,0:T(2,128)} %param.8) | copy-start | bytes 3076
  86.4 53.9 %all-to-all-start.1 = ((bf16[1,16,32,2048]{3,2,0,1:T(8,128)(2,1)}), bf16[1,16,32,2048]{3,2,0,1:T(8,128)(2,1)}, u32[]{:S(2)}, u32[]{:S(2)}) async-start(bf16[1,16,32,2048]{3,2,0,1:T(8,128)(2,1)} %bitcast.50), calls=%async_computation.1 | async-start | bytes 4194304 | tf_op jit(solution)/shard_map/all_to_all | solution.py:46
  146.9 4.9 %copy-start.2 = (bf16[1,128,2048]{2,1,0:T(8,128)(2,1)S(1)}, bf16[1,128,2048]{2,1,0:T(8,128)(2,1)}, u32[]{:S(2)}) copy-start(bf16[1,128,2048]{2,1,0:T(8,128)(2,1)} %param.6) | copy-start | bytes 1572868
  151.9 16.6 %collective-permute-start = (bf16[128,2048]{1,0:T(8,128)(2,1)S(1)}, bf16[128,2048]{1,0:T(8,128)(2,1)S(1)}, u32[]{:S(2)}, u32[]{:S(2)}) collective-permute-start(bf16[128,2048]{1,0:T(8,128)(2,1)S(1)} %add_convert_fusion), channel_id=1, source_target_pairs={{0,128},{128,256},{256,384},{384,512},{512,640},{640,768},{768,896... | collective-permute-start | bytes 1572872 | tf_op jit(solution)/shard_map/ppermute | solution.py:10
where the time goes:
time: 170 us; the launch traced here: 169 us
  blocking collectives  66.6 us (39%)
  waiting for transfers between devices  61.9 us (36%)
  local copies, waits for them, and re-layouts  17.9 us (11%)
  starting transfers between devices  7.46 us (4%)
  other arithmetic  7.3 us (4%)
  matrix products  7.3 us (4%)
    all_to_all x1, blocking collectives, per_device(): lax.all_to_all(outgoing, 'expert', split_axis=0, concat_axis=2, tiled=True)  66.6 us
    all_to_all x1, waiting for transfers between devices, per_device(): lax.all_to_all(expert_out, 'expert', split_axis=1, concat_axis=0, tiled=T...  49 us
    ppermute x1, waiting for transfers between devices, passed_along(): lax.ppermute(value, axis, [(source, source + steps) for source in range(l...  13 us
    scatter x1, local copies, waits for them, and re-layouts, per_device(): outgoing = jnp.zeros((expert_count * capacity, width), jnp.bfloat16).at[s...  7.38 us
    dot_general x1, matrix products, per_device(): jnp.einsum('esf,efd->esd', hidden, expert_down[0], preferred_element_type...  6.06 us
    reduce_sum x1, other arithmetic, per_device(): routed = jnp.sum(picked.reshape(tok_count, top_count, width), axis=1)  4.86 us
    all_to_all x1, starting transfers between devices, per_device(): lax.all_to_all(expert_out, 'expert', split_axis=1, concat_axis=0, tiled=T...  4.75 us
    gather x1, local copies, waits for them, and re-layouts, per_device(): picked = back_rows[slot_index].astype(jnp.float32) * flat_weights[:, None]  4.22 us
  transfers between devices with their start and end apart: 2, of which 2 were waited for; matrix products, arithmetic and copies ran while one was open for 1% of the time, Pallas kernels for 0%

commit v1 on v0

v1 whole, which is shorter than its diff:
```python
import functools

import jax
import jax.numpy as jnp
from jax import lax
from jax.experimental import pallas as pl
from jax.experimental.pallas import tpu as pltpu
from jax.sharding import PartitionSpec as P

MESH = pl.DeviceIdType.MESH
CHIPS = 8
SENDS = 7
UP, DOWN = 0, 1


def kernel(
    tok_hbm, meta_hbm, gate_hbm, up_hbm, down_hbm,
    out_ref, next_ref,
    gath, meta, w_gate, w_up, w_down, contrib, rs_in, rs_out,
    local_sem, w_sem, w_send, w_recv,
    ag_send, ag_recv, meta_send, meta_recv, rs_send, rs_recv, hand_send, hand_recv,
):
    expert = lax.axis_index("expert")
    section = lax.axis_index("section")
    n_expert = 2 * CHIPS
    n_section = lax.axis_size("section")
    core = lax.rem(expert, 2)
    partner = expert + 1 - 2 * core
    neighbour = (
        {"expert": lax.rem(expert + 2, n_expert)},
        {"expert": lax.rem(expert + n_expert - 2, n_expert)},
    )
    after = {"section": lax.rem(section + 1, n_section)}
    before = {"section": lax.rem(section + n_section - 1, n_section)}
    half_rows = gath.shape[2]
    piece_rows = half_rows // 2

    own_tok = [
        pltpu.make_async_copy(
            tok_hbm.at[pl.ds(h * half_rows, half_rows)], gath.at[h, 0], local_sem.at[h]
        )
        for h in range(2)
    ]
    own_meta = pltpu.make_async_copy(meta_hbm, meta.at[0], local_sem.at[2])
    pairs = ((gate_hbm, w_gate), (up_hbm, w_up), (down_hbm, w_down))
    own_w = [
        pltpu.make_async_copy(src, dst.at[0], w_sem.at[i]) for i, (src, dst) in enumerate(pairs)
    ]
    for copy in own_tok + [own_meta] + own_w:
        copy.start()

    barrier = pltpu.get_barrier_semaphore()
    for device in (*neighbour, {"expert": partner}, after, before):
        pl.semaphore_signal(barrier, inc=1, device_id=device, device_id_type=MESH)
    pl.semaphore_wait(barrier, 5)

    def piece(ref, half, slot, part):
        return ref.at[half, slot, pl.ds(part * piece_rows, piece_rows)]

    def ag_copy(half, way, t):
        hop = t // 2
        if way == UP:
            part, source, target = t % 2, hop, hop + 1
        else:
            part, source, target = 1 - t % 2, (CHIPS - hop) % CHIPS, CHIPS - 1 - hop
        return pltpu.make_async_remote_copy(
            src_ref=piece(gath, half, source, part),
            dst_ref=piece(gath, half, target, part),
            send_sem=ag_send.at[half, way, t],
            recv_sem=ag_recv.at[half, target, part],
            device_id=neighbour[way],
            device_id_type=MESH,
        )

    def ag_wait(half, slot, part):
        ref = piece(gath, half, slot, part)
        pltpu.make_async_copy(ref, ref, ag_recv.at[half, slot, part]).wait()

    def ag_event(half, way, t):
        hop = t // 2
        if hop > 0:
            if way == UP:
                ag_wait(half, hop, t % 2)
            else:
                ag_wait(half, CHIPS - hop, 1 - t % 2)
        ag_copy(half, way, t).start()

    def meta_copy(way, hop):
        source, target = (hop, hop + 1) if way == UP else ((CHIPS - hop) % CHIPS, CHIPS - 1 - hop)
        return pltpu.make_async_remote_copy(
            src_ref=meta.at[source],
            dst_ref=meta.at[target],
            send_sem=meta_send.at[way, hop],
            recv_sem=meta_recv.at[target],
            device_id=neighbour[way],
            device_id_type=MESH,
        )

    def meta_wait(slot):
        pltpu.make_async_copy(meta.at[slot], meta.at[slot], meta_recv.at[slot]).wait()

    def meta_event(way, hop):
        if hop > 0:
            meta_wait(hop if way == UP else CHIPS - hop)
        meta_copy(way, hop).start()

    def w_copy(i):
        src, dst = pairs[i]
        return pltpu.make_async_remote_copy(
            src_ref=src,
            dst_ref=dst.at[1],
            send_sem=w_send.at[i],
            recv_sem=w_recv.at[i],
            device_id={"expert": partner},
            device_id_type=MESH,
        )

    own_tok[0].wait()
    own_meta.wait()
    for t in range(SENDS):
        for way in (UP, DOWN):
            ag_event(0, way, t)
            if way == UP and t % 2 == 0:
                meta_event(UP, t // 2)
            if way == DOWN and t % 2 == 1:
                meta_event(DOWN, t // 2)
        if t == 1:
            for i in range(3):
                w_copy(i).start()
            own_tok[1].wait()
    for copy in own_w:
        copy.wait()

    def rs_place(way, t):
        first = 1 if way == UP else 0
        if t == SENDS - 1:
            return 1 - first, 1, t - 1
        if t % 2 == 0:
            return first, 3 - t // 2, t - 2
        return 1 - first, 4 - t // 2, t - 2

    def rs_copy(half, way, t):
        return pltpu.make_async_remote_copy(
            src_ref=rs_out.at[half, way, t],
            dst_ref=rs_in.at[half, way, t],
            send_sem=rs_send.at[half, way, t],
            recv_sem=rs_recv.at[half, way, t],
            device_id=neighbour[way],
            device_id_type=MESH,
        )

    def rs_event(half, way, t):
        part, distance, previous = rs_place(way, t)
        slot = CHIPS - distance if way == UP else distance
        value = contrib[half, slot, pl.ds(part * piece_rows, piece_rows)]
        if previous >= 0:
            rs_copy(half, way, previous).wait_recv()
            value = value + rs_in[half, way, previous].astype(jnp.float32)
        rs_out[half, way, t] = value.astype(jnp.bfloat16)
        rs_copy(half, way, t).start()

    def column(slot, half, own):
        facts = meta[slot]
        weight = jnp.where(facts[0:1] == own, facts[2:3], 0.0) + jnp.where(
            facts[1:2] == own, facts[3:4], 0.0
        )
        shape = (half_rows, 2 * half_rows)
        row = lax.broadcasted_iota(jnp.int32, shape, 0) + half * half_rows
        lane = lax.broadcasted_iota(jnp.int32, shape, 1)
        spread = jnp.where(row == lane, jnp.broadcast_to(weight, shape), 0.0)
        return jnp.sum(spread, axis=1, keepdims=True)

    def compute(half, step):
        pair = lax.div(step, 2)
        which = lax.rem(step, 2)
        base = jnp.where(pair == 0, 0, jnp.where(pair == 1, 6, 2 * pair - 2))
        own = jnp.where(which == 0, expert, partner).astype(jnp.float32)
        rows = gath[half, pl.ds(base, 2)]
        rows = rows.reshape(2 * half_rows, rows.shape[2])
        gate_val = jnp.dot(rows, w_gate[which], preferred_element_type=jnp.float32)
        up_val = jnp.dot(rows, w_up[which], preferred_element_type=jnp.float32)
        hidden = (gate_val / (1.0 + jnp.exp(-gate_val)) * up_val).astype(jnp.bfloat16)
        result = jnp.dot(hidden, w_down[which], preferred_element_type=jnp.float32)

        for i in range(2):
            scaled = result[i * half_rows:(i + 1) * half_rows] * column(base + i, half, own)

            @pl.when(which == 0)
            def _():
                contrib[half, base + i] = scaled

            @pl.when(which == 1)
            def _():
                contrib[half, base + i] = contrib[half, base + i] + scaled

    @pl.loop(0, 16)
    def _(step):
        half = lax.div(step, 8)
        inner = lax.rem(step, 8)
        for t in range(SENDS):

            @pl.when(step == t)
            def _():
                for way in (UP, DOWN):
                    ag_event(1, way, t)

            @pl.when(step == 8 + t)
            def _():
                for way in (UP, DOWN):
                    rs_event(0, way, t)

        @pl.when(step == 1)
        def _():
            for i in range(3):
                w_copy(i).wait_recv()

        for h in range(2):

            @pl.when(step == 8 * h + 4)
            def _():
                ag_wait(h, 3, 1)

            @pl.when(step == 8 * h + 6)
            def _():
                ag_wait(h, 5, 0)
                ag_wait(h, 4, 0)
                ag_wait(h, 4, 1)

        @pl.when(step == 6)
        def _():
            meta_wait(4)
            meta_wait(5)

        compute(half, inner)

    def hand_copy(half):
        rows = pl.ds(half * half_rows, half_rows)
        return pltpu.make_async_remote_copy(
            src_ref=out_ref.at[rows],
            dst_ref=next_ref.at[rows],
            send_sem=hand_send.at[half],
            recv_sem=hand_recv.at[half],
            device_id=after,
            device_id_type=MESH,
        )

    def finish(half):
        for t in (4, 6):
            for way in (UP, DOWN):
                rs_copy(half, way, t).wait_recv()
        for part in range(2):
            rows = pl.ds(part * piece_rows, piece_rows)
            upward = rs_in[half, UP, 6 - 2 * part].astype(jnp.float32)
            downward = rs_in[half, DOWN, 4 + 2 * part].astype(jnp.float32)
            routed = contrib[half, 0, rows] + (upward + downward)
            total = gath[half, 0, rows].astype(jnp.float32) + routed
            out_ref[pl.ds(half * half_rows + part * piece_rows, piece_rows)] = total.astype(
                jnp.bfloat16
            )
        hand_copy(half).start()

    for t in range(SENDS):
        for way in (UP, DOWN):
            rs_event(1, way, t)
        if t == 1:
            finish(0)
    finish(1)

    for half in range(2):
        for way in (UP, DOWN):
            for t in range(SENDS):
                ag_copy(half, way, t).wait_send()
                rs_copy(half, way, t).wait_send()
    for way in (UP, DOWN):
        for hop in range(4 - way):
            meta_copy(way, hop).wait_send()
    for i in range(3):
        w_copy(i).wait_send()
    for half in range(2):
        hand_copy(half).wait()

    @pl.when(section == 0)
    def _():
        next_ref[...] = jnp.zeros_like(next_ref)


def per_device(tokens, routes, route_weights, expert_gate, expert_up, expert_down):
    rows_in = tokens[0]
    tok_count, width = rows_in.shape
    hidden = expert_gate.shape[3]
    facts = jnp.concatenate(
        [
            routes[0].astype(jnp.float32).T,
            route_weights[0].T,
            jnp.zeros((4, tok_count), jnp.float32),
        ]
    )
    half = tok_count // 2
    result = jax.ShapeDtypeStruct((tok_count, width), jnp.bfloat16)
    dma = pltpu.SemaphoreType.DMA
    layer_out, handed = pl.pallas_call(
        kernel,
        out_shape=(result, result),
        in_specs=[pl.BlockSpec(memory_space=pl.ANY)] * 5,
        out_specs=(pl.BlockSpec(memory_space=pltpu.VMEM),) * 2,
        scratch_shapes=[
            pltpu.VMEM((2, CHIPS, half, width), jnp.bfloat16),
            pltpu.VMEM((CHIPS, 8, tok_count), jnp.float32),
            pltpu.VMEM((2, width, hidden), jnp.bfloat16),
            pltpu.VMEM((2, width, hidden), jnp.bfloat16),
            pltpu.VMEM((2, hidden, width), jnp.bfloat16),
            pltpu.VMEM((2, CHIPS, half, width), jnp.float32),
            pltpu.VMEM((2, 2, SENDS, half // 2, width), jnp.bfloat16),
            pltpu.VMEM((2, 2, SENDS, half // 2, width), jnp.bfloat16),
            dma((3,)),
            dma((3,)),
            dma((3,)),
            dma((3,)),
            dma((2, 2, SENDS)),
            dma((2, CHIPS, 2)),
            dma((2, 4)),
            dma((CHIPS,)),
            dma((2, 2, SENDS)),
            dma((2, 2, SENDS)),
            dma((2,)),
            dma((2,)),
        ],
        compiler_params=pltpu.CompilerParams(
            collective_id=0, has_side_effects=True, vmem_limit_bytes=60 * 1024 * 1024
        ),
    )(rows_in, facts, expert_gate[0, 0], expert_up[0, 0], expert_down[0, 0])
    return (layer_out[None], handed[None])


def solution(mesh):
    in_specs = (
        P("section", ("expert", "tensor"), None),
        P("section", ("expert", "tensor"), None),
        P("section", ("expert", "tensor"), None),
        P("section", "expert", None, None),
        P("section", "expert", None, None),
        P("section", "expert", None, None),
    )
    out_specs = (P("section", ("expert", "tensor"), None), P("section", ("expert", "tensor"), None))
    return jax.shard_map(
        per_device, mesh=mesh, in_specs=in_specs, out_specs=out_specs, check_vma=False
    )
```

time: 170 us -> 120 us (0.71)
  the two profiles are of different devices: /device:TPU:64 before, /device:TPU:2 now
where the time goes in v1:
time: 120 us
  Pallas kernels  114 us (95%)
  local copies, waits for them, and re-layouts  3.84 us (3%)
  other arithmetic  2.02 us (2%)
    pallas_call x1, Pallas kernels, per_device(): pl.pallas_call(kernel, out_shape=(result, result), in_specs=[pl.BlockSpec...  114 us
    unnamed x2, local copies, waits for them, and re-layouts  3.76 us

profile of v1, /device:TPU:2, one launch (start us, length us, event | category | flops | bytes accessed | tf_op | source)
XLA Modules:
  0.0 120.2 jit_solution(15775796882771169507)
XLA Ops:
  0.6 0.1 pad.2.clone
  0.7 0.7 convert_bitcast_fusion
  1.4 1.3 %maximum_maximum_fusion.meta_hbm = f32[8,128]{1,0:T(8,128)} fusion(f32[2,128]{1,0:T(2,128)} %bitcast.19, f32[2,128]{1,0:T(2,128)S(1)} %convert_bitcast_fusion, f32[8]{0:T(128)S(1)} %pad.2.clone), kind=kLoop, calls=%fused_computation | loop fusion | flops 2048 | bytes 6176 | tf_op jit(solution)/shard_map/concatenate | solution.py:291
  2.7 113.7 %shard_map.77 = (bf16[128,2048]{1,0:T(8,128)(2,1)}, bf16[128,2048]{1,0:T(8,128)(2,1)}) custom-call(bf16[128,2048]{1,0:T(8,128)(2,1)} %bitcast.16, f32[8,128]{1,0:T(8,128)} %maximum_maximum_fusion.meta_hbm, bf16[2048,512]{1,0:T(8,128)(2,1)} %bitcast.13, bf16[2048,512]{1,0:T(8,128)(2,1)} %bitcast.14, bf16[512,2048]{1,0:T(8,128)(2,1)} %bitcast.15), custom_call_target="tpu_custom_call" | custom-call | tf_op jit(solution)/shard_map/pallas_call | solution.py:301
  116.4 1.9 %copy.10 = bf16[1,128,2048]{2,1,0:T(8,128)(2,1)} copy(bf16[1,128,2048]{2,1,0:T(8,128)(2,1)} %bitcast.18) | data formatting | bytes 1048576
  118.3 1.9 %copy.11 = bf16[1,128,2048]{2,1,0:T(8,128)(2,1)} copy(bf16[1,128,2048]{2,1,0:T(8,128)(2,1)} %bitcast.17) | data formatting | bytes 1048576
  (1 shorter events, 0.0 us)

commit v2 on v1

--- a/solution.py
+++ b/solution.py
@@ -11,10 +11,11 @@
 CHIPS = 8
 SENDS = 7
 UP, DOWN = 0, 1
+PARTS = 4
 
 
 def kernel(
-    tok_hbm, meta_hbm, gate_hbm, up_hbm, down_hbm,
+    tok_hbm, routes_ref, weights_ref, gate_hbm, up_hbm, down_hbm,
     out_ref, next_ref,
     gath, meta, w_gate, w_up, w_down, contrib, rs_in, rs_out,
     local_sem, w_sem, w_send, w_recv,
@@ -41,13 +42,15 @@
         )
         for h in range(2)
     ]
-    own_meta = pltpu.make_async_copy(meta_hbm, meta.at[0], local_sem.at[2])
     pairs = ((gate_hbm, w_gate), (up_hbm, w_up), (down_hbm, w_down))
     own_w = [
         pltpu.make_async_copy(src, dst.at[0], w_sem.at[i]) for i, (src, dst) in enumerate(pairs)
     ]
-    for copy in own_tok + [own_meta] + own_w:
+    for copy in own_tok + own_w:
         copy.start()
+    meta[0, 0:2] = routes_ref[...].astype(jnp.float32)
+    meta[0, 2:4] = weights_ref[...]
+    meta[0, 4:8] = jnp.zeros((4, meta.shape[2]), jnp.float32)
 
     barrier = pltpu.get_barrier_semaphore()
     for device in (*neighbour, {"expert": partner}, after, before):
@@ -116,7 +119,6 @@
         )
 
     own_tok[0].wait()
-    own_meta.wait()
     for t in range(SENDS):
         for way in (UP, DOWN):
             ag_event(0, way, t)
@@ -173,7 +175,7 @@
     def compute(half, step):
         pair = lax.div(step, 2)
         which = lax.rem(step, 2)
-        base = jnp.where(pair == 0, 0, jnp.where(pair == 1, 6, 2 * pair - 2))
+        base = jnp.where(pair == 0, 6, jnp.where(pair == 3, 0, 2 * pair))
         own = jnp.where(which == 0, expert, partner).astype(jnp.float32)
         rows = gath[half, pl.ds(base, 2)]
         rows = rows.reshape(2 * half_rows, rows.shape[2])
@@ -204,10 +206,17 @@
                 for way in (UP, DOWN):
                     ag_event(1, way, t)
 
-            @pl.when(step == 8 + t)
+            @pl.when(step == 7 + t)
             def _():
                 for way in (UP, DOWN):
                     rs_event(0, way, t)
+
+        for t in range(2):
+
+            @pl.when(step == 14 + t)
+            def _():
+                for way in (UP, DOWN):
+                    rs_event(1, way, t)
 
         @pl.when(step == 1)
         def _():
@@ -216,17 +225,17 @@
 
         for h in range(2):
 
+            @pl.when(step == 8 * h + 2)
+            def _():
+                ag_wait(h, 3, 1)
+
             @pl.when(step == 8 * h + 4)
-            def _():
-                ag_wait(h, 3, 1)
-
-            @pl.when(step == 8 * h + 6)
             def _():
                 ag_wait(h, 5, 0)
                 ag_wait(h, 4, 0)
                 ag_wait(h, 4, 1)
 
-        @pl.when(step == 6)
+        @pl.when(step == 4)
         def _():
             meta_wait(4)
             meta_wait(5)
@@ -259,11 +268,10 @@
             )
         hand_copy(half).start()
 
-    for t in range(SENDS):
+    finish(0)
+    for t in range(2, SENDS):
         for way in (UP, DOWN):
             rs_event(1, way, t)
-        if t == 1:
-            finish(0)
     finish(1)
 
     for half in range(2):
@@ -284,24 +292,38 @@
         next_ref[...] = jnp.zeros_like(next_ref)
 
 
+def place(layer_ref, hand_ref, layer_out, hand_out, held, in_sem, out_sem):
+    ends = ((layer_ref, layer_out), (hand_ref, hand_out))
+    rows = layer_ref.shape[0] // PARTS
+    inward, outward = [], []
+    for part in range(PARTS):
+        where = pl.ds(part * rows, rows)
+        for i, (source, target) in enumerate(ends):
+            block = held.at[i, where]
+            inward.append(pltpu.make_async_copy(source.at[where], block, in_sem.at[i, part]))
+            outward.append(pltpu.make_async_copy(block, target.at[where], out_sem.at[i, part]))
+    for copy in inward:
+        copy.start()
+    for arrival, departure in zip(inward, outward):
+        arrival.wait()
+        departure.start()
+    for copy in outward:
+        copy.wait()
+
+
 def per_device(tokens, routes, route_weights, expert_gate, expert_up, expert_down):
     rows_in = tokens[0]
     tok_count, width = rows_in.shape
     hidden = expert_gate.shape[3]
-    facts = jnp.concatenate(
-        [
-            routes[0].astype(jnp.float32).T,
-            route_weights[0].T,
-            jnp.zeros((4, tok_count), jnp.float32),
-        ]
-    )
     half = tok_count // 2
     result = jax.ShapeDtypeStruct((tok_count, width), jnp.bfloat16)
     dma = pltpu.SemaphoreType.DMA
     layer_out, handed = pl.pallas_call(
         kernel,
         out_shape=(result, result),
-        in_specs=[pl.BlockSpec(memory_space=pl.ANY)] * 5,
+        in_specs=[pl.BlockSpec(memory_space=pl.ANY)]
+        + [pl.BlockSpec(memory_space=pltpu.VMEM)] * 2
+        + [pl.BlockSpec(memory_space=pl.ANY)] * 3,
         out_specs=(pl.BlockSpec(memory_space=pltpu.VMEM),) * 2,
         scratch_shapes=[
             pltpu.VMEM((2, CHIPS, half, width), jnp.bfloat16),
@@ -312,7 +334,7 @@
             pltpu.VMEM((2, CHIPS, half, width), jnp.float32),
             pltpu.VMEM((2, 2, SENDS, half // 2, width), jnp.bfloat16),
             pltpu.VMEM((2, 2, SENDS, half // 2, width), jnp.bfloat16),
-            dma((3,)),
+            dma((2,)),
             dma((3,)),
             dma((3,)),
             dma((3,)),
@@ -328,7 +350,25 @@
         compiler_params=pltpu.CompilerParams(
             collective_id=0, has_side_effects=True, vmem_limit_bytes=60 * 1024 * 1024
         ),
-    )(rows_in, facts, expert_gate[0, 0], expert_up[0, 0], expert_down[0, 0])
+    )(
+        rows_in,
+        routes[0].T,
+        route_weights[0].T,
+        expert_gate[0, 0],
+        expert_up[0, 0],
+        expert_down[0, 0],
+    )
+    layer_out, handed = pl.pallas_call(
+        place,
+        out_shape=(result, result),
+        in_specs=[pl.BlockSpec(memory_space=pl.ANY)] * 2,
+        out_specs=(pl.BlockSpec(memory_space=pl.ANY),) * 2,
+        scratch_shapes=[
+            pltpu.VMEM((2, tok_count, width), jnp.bfloat16),
+            dma((2, PARTS)),
+            dma((2, PARTS)),
+        ],
+    )(layer_out, handed)
     return (layer_out[None], handed[None])
 
 

time: 120 us -> 115 us (0.958)
  local copies, waits for them, and re-layouts: 3.84 us -> 0 us
  other arithmetic: 2.02 us -> 0 us
    unnamed x2 -> x0, local copies, waits for them, and re-layouts: 3.76 us -> none
    pallas_call x0 -> x1, Pallas kernels: none -> 2.09 us  [per_device(): pl.pallas_call(place, out_shape=(result, result), in_specs=[pl.BlockSpec(...]
    pallas_call x1, Pallas kernels: 114 us -> 112 us  [per_device(): pl.pallas_call(kernel, out_shape=(result, result), in_specs=[pl.BlockSpec...]
    concatenate x1 -> x0, other arithmetic: 1.34 us -> none  [per_device(): jnp.concatenate([routes[0].astype(jnp.float32).T, route_weights[0].T, jnp...]
where the time goes in v2:
time: 115 us; the launch traced here: 114 us
  Pallas kernels  114 us (99%)
    pallas_call x1, Pallas kernels, per_device(): pl.pallas_call(kernel, out_shape=(result, result), in_specs=[pl.BlockSpec...  112 us

profile of v2, /device:TPU:2, one launch (start us, length us, event | category | flops | bytes accessed | tf_op | source)
XLA Modules:
  0.0 114.5 jit_solution(16859462344866895100)
XLA Ops:
  0.6 111.7 %shard_map.77 = (bf16[128,2048]{1,0:T(8,128)(2,1)}, bf16[128,2048]{1,0:T(8,128)(2,1)}) custom-call(bf16[128,2048]{1,0:T(8,128)(2,1)} %bitcast.15, s32[2,128]{1,0:T(2,128)} %bitcast.16, f32[2,128]{1,0:T(2,128)} %bitcast.17, bf16[2048,512]{1,0:T(8,128)(2,1)} %bitcast.12, bf16[2048,512]{1,0:T(8,128)(2,1)} %bitcast.13, bf16[512,2048]{1,0:T(8,128)(2,1)} %bitcast.14), custom_call_target="tpu_custom_call" | custom-call | tf_op jit(solution)/shard_map/pallas_call | solution.py:321
  112.4 2.1 %shard_map.78 = (bf16[128,2048]{1,0:T(8,128)(2,1)}, bf16[128,2048]{1,0:T(8,128)(2,1)}) custom-call(bf16[128,2048]{1,0:T(8,128)(2,1)} %get-tuple-element.6.layer_ref, bf16[128,2048]{1,0:T(8,128)(2,1)} %get-tuple-element.7.hand_ref), custom_call_target="tpu_custom_call" | custom-call | tf_op jit(solution)/shard_map/pallas_call | solution.py:361

commit v3 on v2

--- a/solution.py
+++ b/solution.py
@@ -12,6 +12,7 @@
 SENDS = 7
 UP, DOWN = 0, 1
 PARTS = 4
+LAG = 5
 
 
 def kernel(
@@ -141,25 +142,32 @@
             return first, 3 - t // 2, t - 2
         return 1 - first, 4 - t // 2, t - 2
 
-    def rs_copy(half, way, t):
+    def rs_rows(half, sub):
+        count = piece_rows // (1 + half)
+        return sub * count, count
+
+    def rs_copy(half, way, t, sub=0):
+        rows = pl.ds(*rs_rows(half, sub))
         return pltpu.make_async_remote_copy(
-            src_ref=rs_out.at[half, way, t],
-            dst_ref=rs_in.at[half, way, t],
-            send_sem=rs_send.at[half, way, t],
-            recv_sem=rs_recv.at[half, way, t],
+            src_ref=rs_out.at[half, way, t, rows],
+            dst_ref=rs_in.at[half, way, t, rows],
+            send_sem=rs_send.at[half + sub, way, t],
+            recv_sem=rs_recv.at[half + sub, way, t],
             device_id=neighbour[way],
             device_id_type=MESH,
         )
 
-    def rs_event(half, way, t):
+    def rs_event(half, way, t, sub=0):
         part, distance, previous = rs_place(way, t)
         slot = CHIPS - distance if way == UP else distance
-        value = contrib[half, slot, pl.ds(part * piece_rows, piece_rows)]
+        start, count = rs_rows(half, sub)
+        rows = pl.ds(start, count)
+        value = contrib[half, slot, pl.ds(part * piece_rows + start, count)]
         if previous >= 0:
-            rs_copy(half, way, previous).wait_recv()
-            value = value + rs_in[half, way, previous].astype(jnp.float32)
-        rs_out[half, way, t] = value.astype(jnp.bfloat16)
-        rs_copy(half, way, t).start()
+            rs_copy(half, way, previous, sub).wait_recv()
+            value = value + rs_in[half, way, previous, rows].astype(jnp.float32)
+        rs_out[half, way, t, rows] = value.astype(jnp.bfloat16)
+        rs_copy(half, way, t, sub).start()
 
     def column(slot, half, own):
         facts = meta[slot]
@@ -242,50 +250,60 @@
 
         compute(half, inner)
 
-    def hand_copy(half):
-        rows = pl.ds(half * half_rows, half_rows)
+    def hand_copy(half, part, sub=0):
+        start, count = rs_rows(half, sub)
+        rows = pl.ds(half * half_rows + part * piece_rows + start, count)
         return pltpu.make_async_remote_copy(
             src_ref=out_ref.at[rows],
             dst_ref=next_ref.at[rows],
-            send_sem=hand_send.at[half],
-            recv_sem=hand_recv.at[half],
+            send_sem=hand_send.at[half + sub, part],
+            recv_sem=hand_recv.at[half + sub, part],
             device_id=after,
             device_id_type=MESH,
         )
 
-    def finish(half):
+    def finish(half, sub=0):
         for t in (4, 6):
             for way in (UP, DOWN):
-                rs_copy(half, way, t).wait_recv()
+                rs_copy(half, way, t, sub).wait_recv()
+        start, count = rs_rows(half, sub)
         for part in range(2):
-            rows = pl.ds(part * piece_rows, piece_rows)
-            upward = rs_in[half, UP, 6 - 2 * part].astype(jnp.float32)
-            downward = rs_in[half, DOWN, 4 + 2 * part].astype(jnp.float32)
+            rows = pl.ds(part * piece_rows + start, count)
+            upward = rs_in[half, UP, 6 - 2 * part, pl.ds(start, count)].astype(jnp.float32)
+            downward = rs_in[half, DOWN, 4 + 2 * part, pl.ds(start, count)].astype(jnp.float32)
             routed = contrib[half, 0, rows] + (upward + downward)
             total = gath[half, 0, rows].astype(jnp.float32) + routed
-            out_ref[pl.ds(half * half_rows + part * piece_rows, piece_rows)] = total.astype(
+            out_ref[pl.ds(half * half_rows + part * piece_rows + start, count)] = total.astype(
                 jnp.bfloat16
             )
-        hand_copy(half).start()
+            hand_copy(half, part, sub).start()
 
     finish(0)
-    for t in range(2, SENDS):
+    for t in range(2, SENDS + LAG):
         for way in (UP, DOWN):
-            rs_event(1, way, t)
-    finish(1)
+            if t < SENDS:
+                rs_event(1, way, t, 0)
+            if t >= LAG:
+                rs_event(1, way, t - LAG, 1)
+        if t == SENDS:
+            finish(1, 0)
+    finish(1, 1)
 
     for half in range(2):
         for way in (UP, DOWN):
             for t in range(SENDS):
                 ag_copy(half, way, t).wait_send()
-                rs_copy(half, way, t).wait_send()
+                for sub in range(1 + half):
+                    rs_copy(half, way, t, sub).wait_send()
     for way in (UP, DOWN):
         for hop in range(4 - way):
             meta_copy(way, hop).wait_send()
     for i in range(3):
         w_copy(i).wait_send()
     for half in range(2):
-        hand_copy(half).wait()
+        for sub in range(1 + half):
+            for part in range(2):
+                hand_copy(half, part, sub).wait()
 
     @pl.when(section == 0)
     def _():
@@ -342,10 +360,10 @@
             dma((2, CHIPS, 2)),
             dma((2, 4)),
             dma((CHIPS,)),
-            dma((2, 2, SENDS)),
-            dma((2, 2, SENDS)),
-            dma((2,)),
-            dma((2,)),
+            dma((3, 2, SENDS)),
+            dma((3, 2, SENDS)),
+            dma((3, 2)),
+            dma((3, 2)),
         ],
         compiler_params=pltpu.CompilerParams(
             collective_id=0, has_side_effects=True, vmem_limit_bytes=60 * 1024 * 1024

time: 115 us -> 119 us (1.035)
  Pallas kernels: 114 us -> 118 us
    pallas_call x1, Pallas kernels: 112 us -> 116 us  [per_device(): pl.pallas_call(kernel, out_shape=(result, result), in_specs=[pl.BlockSpec...]
where the time goes in v3:
time: 119 us; the launch traced here: 118 us
  Pallas kernels  118 us (99%)
    pallas_call x1, Pallas kernels, per_device(): pl.pallas_call(kernel, out_shape=(result, result), in_specs=[pl.BlockSpec...  116 us

profile of v3, /device:TPU:2, one launch (start us, length us, event | category | flops | bytes accessed | tf_op | source)
XLA Modules:
  0.0 118.5 jit_solution(3744071726980270666)
XLA Ops:
  0.6 115.8 %shard_map.77 = (bf16[128,2048]{1,0:T(8,128)(2,1)}, bf16[128,2048]{1,0:T(8,128)(2,1)}) custom-call(bf16[128,2048]{1,0:T(8,128)(2,1)} %bitcast.15, s32[2,128]{1,0:T(2,128)} %bitcast.16, f32[2,128]{1,0:T(2,128)} %bitcast.17, bf16[2048,512]{1,0:T(8,128)(2,1)} %bitcast.12, bf16[2048,512]{1,0:T(8,128)(2,1)} %bitcast.13, bf16[512,2048]{1,0:T(8,128)(2,1)} %bitcast.14), custom_call_target="tpu_custom_call" | custom-call | tf_op jit(solution)/shard_map/pallas_call | solution.py:339
  116.4 2.1 %shard_map.78 = (bf16[128,2048]{1,0:T(8,128)(2,1)}, bf16[128,2048]{1,0:T(8,128)(2,1)}) custom-call(bf16[128,2048]{1,0:T(8,128)(2,1)} %get-tuple-element.6.layer_ref, bf16[128,2048]{1,0:T(8,128)(2,1)} %get-tuple-element.7.hand_ref), custom_call_target="tpu_custom_call" | custom-call | tf_op jit(solution)/shard_map/pallas_call | solution.py:379
